TPU v7x, 32 devices: a whole 2x2x4 slice. The times are simulated.
32 devices in a mesh: proto: 8 (over z, x), design: 4 (over y, core).
Axes of the slice: x: 2, y: 2, z: 4, core: 2. Of those that a mesh axis runs over, the one named last changes fastest.
Arguments:
- designs: bfloat16 [32768, 1024], P(('proto', 'design')), may hold values from -32 to 32
- prototypes: float32 [16384, 1024], P('proto'), may hold values from -6 to 6
- candidates: int32 [32, 24], P(('proto', 'design')), may hold values from 0 to 127, as said below
- positives: int32 [32768], P(('proto', 'design')), may hold values from 0 to 16383, as said below
Outputs:
- losses: float32 [32768], P(('proto', 'design'))
- design_grad: bfloat16 [32768, 1024], P(('proto', 'design'))
- proto_grad: float32 [16384, 1024], P(('proto', 'design'))
Inputs may be any that keep to these rules, and one draw needn't show every extreme that they name: `candidates`: row g lists 24 distinct blocks for the designs of device g along proto+design. Block b lies in proto shard b // 16; at most 4 blocks of a row lie in one proto shard, and in every draw one shard holds exactly 4 blocks of every row. `positives`: the positive row of design i lies in one of the blocks of row i // 1024 of candidates.
All inputs are finite; a program needn't handle non-finite values.
Results may differ from a plain program's by a relative error of at most 0.0062.
Values may be sent and summed in bfloat16 or wider, within the bound.
No kernel may reach another device: no remote copies, remote signals or barrier semaphores. Data moves between devices by JAX's collectives and lax.ppermute only.
A program may use at most 128 MiB of HBM per device.

v0:
```python
import jax
import jax.numpy as jnp
from jax import lax
from jax.sharding import PartitionSpec as P

D = 1024
TILE = 128


def contrast(design_rows, cand_rows, block_list, positive_ids):
    logit_scale = D ** (-0.5)
    logits = (
        lax.dot_general(
            design_rows, cand_rows, (((1,), (1,)), ((), ())), preferred_element_type=jnp.float32
        )
        * logit_scale
    )
    cand_count = block_list.shape[0]
    block_match = (positive_ids // TILE)[:, None] == block_list[None, :]
    cand_index = jnp.sum(
        jnp.where(block_match, jnp.arange(cand_count, dtype=jnp.int32)[None, :], 0), axis=1
    )
    positive_col = cand_index * TILE + positive_ids % TILE
    columns = jnp.arange(cand_count * TILE, dtype=jnp.int32)
    target = columns[None, :] == positive_col[:, None]
    row_max = jnp.max(logits, axis=1, keepdims=True)
    log_total = row_max + jnp.log(jnp.sum(jnp.exp(logits - row_max), axis=1, keepdims=True))
    picked = jnp.sum(jnp.where(target, logits, 0.0), axis=1)
    losses = log_total[:, 0] - picked
    chances = jnp.exp(logits - log_total)
    logit_grad = (chances - target.astype(jnp.float32)).astype(jnp.bfloat16)
    design_grad = jnp.dot(logit_grad, cand_rows, preferred_element_type=jnp.float32).astype(
        jnp.bfloat16
    )
    return (losses, design_grad, logit_grad)


def slot_plan(block_list, blocks_dev, capacity, proto_count):
    owners = block_list // blocks_dev
    local_ids = block_list % blocks_dev
    cand_count = block_list.shape[0]
    cand_ids = jnp.arange(cand_count, dtype=jnp.int32)
    same_owner = owners[:, None] == owners[None, :]
    earlier = cand_ids[None, :] < cand_ids[:, None]
    rank_of = jnp.sum(jnp.where(same_owner & earlier, 1, 0), axis=1).astype(jnp.int32)
    slot_of = owners * capacity + rank_of
    hit_table = slot_of[None, :] == jnp.arange(proto_count * capacity, dtype=jnp.int32)[:, None]
    requested = jnp.sum(jnp.where(hit_table, local_ids[None, :] + 1, 0), axis=1) - 1
    source = jnp.sum(jnp.where(hit_table, cand_ids[None, :], 0), axis=1)
    filled = jnp.any(hit_table, axis=1)
    return (slot_of, requested, source, filled)


def body(designs, prototypes, candidates, positives):
    proto_count = lax.axis_size("proto")
    cand_count = candidates.shape[1]
    blocks_dev = prototypes.shape[0] // TILE
    feature_width = designs.shape[1]
    design_count = designs.shape[0]
    capacity = max(2, (4 * cand_count + 3 * proto_count - 1) // (3 * proto_count))
    slot_total = proto_count * capacity
    own_list = candidates[0]
    slot_of, requested, source, filled = slot_plan(own_list, blocks_dev, capacity, proto_count)
    everyone = lax.all_gather(designs, "proto", axis=0, tiled=True)
    incoming = lax.all_to_all(requested, "proto", split_axis=0, concat_axis=0, tiled=True)
    proto_table = prototypes.astype(jnp.bfloat16).reshape(blocks_dev, TILE, feature_width)
    fetched = jnp.take(proto_table, jnp.maximum(incoming, 0), axis=0)
    outgoing = jnp.where((incoming >= 0)[:, None, None], fetched, jnp.zeros((), jnp.bfloat16))
    arrived = lax.all_to_all(outgoing, "proto", split_axis=0, concat_axis=0, tiled=True)
    cand_rows = jnp.take(arrived, slot_of, axis=0).reshape(cand_count * TILE, feature_width)
    losses, design_grad, logit_grad = contrast(designs, cand_rows, own_list, positives)
    slab_rows = logit_grad.T.reshape(cand_count, TILE, design_count)
    outgoing_slab = jnp.where(
        filled[:, None, None], jnp.take(slab_rows, source, axis=0), jnp.zeros((), jnp.bfloat16)
    )
    received = lax.all_to_all(outgoing_slab, "proto", split_axis=0, concat_axis=0, tiled=True)
    returned = jnp.einsum(
        "pctb,pbd->pctd",
        received.reshape(proto_count, capacity, TILE, design_count),
        everyone.reshape(proto_count, design_count, feature_width),
        preferred_element_type=jnp.float32,
    )
    selector = (incoming[None, :] == jnp.arange(blocks_dev, dtype=jnp.int32)[:, None]).astype(
        jnp.float32
    )
    summed = jnp.dot(
        selector,
        returned.reshape(slot_total, TILE * feature_width),
        precision=lax.Precision.HIGHEST,
        preferred_element_type=jnp.float32,
    )
    summed = summed.reshape(blocks_dev * TILE, feature_width)
    owned_rows = lax.psum_scatter(summed, "design", scatter_dimension=0, tiled=True)
    return (losses, design_grad, owned_rows)


def solution(mesh):
    return jax.shard_map(
        body,
        mesh=mesh,
        in_specs=(
            P(("proto", "design"), None),
            P("proto", None),
            P(("proto", "design"), None),
            P(("proto", "design")),
        ),
        out_specs=(
            P(("proto", "design")),
            P(("proto", "design"), None),
            P(("proto", "design"), None),
        ),
        check_vma=False,
    )
```

profile of v0, /device:TPU:0, one launch (start us, length us, event | category | flops | bytes accessed | tf_op | source)
XLA Modules:
  0.0 743.1 jit_solution(12302184155922317201)
XLA Ops:
  7.2 0.7 and_select_fusion.3
  7.8 0.7 fusion.22
  8.5 0.2 select_reduce_fusion.3
  8.7 0.1 select_reduce_fusion.1
  8.8 0.7 sub.53
  9.5 7.3 all-to-all-start
  16.7 6.0 convert_element_type.19
  22.7 0.4 all-to-all-done
  23.2 0.5 broadcast.314
  23.7 0.7 fusion.27
  24.5 7.2 gather_fusion
  31.7 7.6 %select_select_fusion.1 = bf16[32,128,1024]{2,1,0:T(8,128)(2,1)} fusion(bf16[32,128,1024]{2,1,0:T(8,128)(2,1)} %gather_fusion, pred[32]{0:T(512)(128)(4,1)S(1)} %get-tuple-element.12, pred[32]{0:T(512)(128)(4,1)S(1)} %get-tuple-element.11), kind=kLoop, calls=%fused_computation.17 | loop fusion | flops 8388608 | bytes 16777280 | tf_op jit(solution)/shard_map/jit(_where)/select_n | solution.py:68
  39.3 5.7 all-to-all-start.1
  45.0 0.7 all-gather.2.cloned.1.call-update
  45.8 0.1 fusion.14
  46.1 341.6 %all-to-all-done.1 = bf16[32,128,1024]{2,1,0:T(8,128)(2,1)} async-done(((bf16[32,128,1024]{2,1,0:T(8,128)(2,1)}), bf16[32,128,1024]{2,1,0:T(8,128)(2,1)}, u32[]{:S(2)}, u32[]{:S(2)}) %all-to-all-start.1) | async-done | bytes 8388640 | tf_op jit(solution)/shard_map/all_to_all | solution.py:69
  387.7 8.1 %gather_fusion.1 = bf16[24,128,1024]{2,1,0:T(8,128)(2,1)} fusion(bf16[32,128,1024]{2,1,0:T(8,128)(2,1)} %all-to-all-done.1, s32[1024]{0:T(1024)S(1)} %pad_clamp_fusion.1), kind=kCustom, calls=%fused_computation.1 | custom fusion | bytes 12583008 | tf_op jit(solution)/shard_map/jit(_take)/gather | solution.py:70
  395.8 4.0 bitcast_select_fusion.1
  399.8 6.8 multiply_reduce_fusion
  406.6 3.6 fusion.2
  410.3 1.1 fusion.28
  411.4 5.1 subtract_convert_fusion
  416.5 7.8 %gather_fusion.2 = bf16[32,128,1024]{2,1,0:T(8,128)(2,1)} fusion(bf16[24,128,1024]{2,1,0:T(8,128)(2,1)} %bitcast.77, s32[1024]{0:T(1024)S(1)} %pad_clamp_fusion), kind=kCustom, calls=%fused_computation.2 | custom fusion | bytes 16777344 | tf_op jit(solution)/shard_map/jit(_take)/gather | solution.py:74
  424.3 7.6 %select_select_fusion = bf16[32,128,1024]{2,1,0:T(8,128)(2,1)} fusion(bf16[32,128,1024]{2,1,0:T(8,128)(2,1)} %gather_fusion.2, pred[32]{0:T(512)(128)(4,1)S(1)} %compare_and_fusion, pred[32]{0:T(512)(128)(4,1)S(1)} %fusion.14), kind=kLoop, calls=%fused_computation.16 | loop fusion | flops 8388608 | bytes 16777280 | tf_op jit(solution)/shard_map/jit(_where)/select_n | solution.py:73
  431.9 5.2 all-to-all-start.2
  437.1 179.5 %all-to-all-done.2 = bf16[32,128,1024]{2,1,0:T(8,128)(2,1)} async-done(((bf16[32,128,1024]{2,1,0:T(8,128)(2,1)}), bf16[32,128,1024]{2,1,0:T(8,128)(2,1)}, u32[]{:S(2)}, u32[]{:S(2)}) %all-to-all-start.2) | async-done | bytes 8388640 | tf_op jit(solution)/shard_map/all_to_all | solution.py:76
  616.6 19.3 %fusion.29 = f32[8,4,128,1024]{3,2,1,0:T(8,128)} fusion(bf16[8,4,128,1024]{3,2,1,0:T(8,128)(2,1)} %bitcast.16, bf16[8,1024,1024,1]{2,1,3,0:T(8,128)(2,1)} %bitcast.80), kind=kOutput, calls=%fused_computation.83 | convolution fusion | flops 8589934592 | bytes 41943040 | tf_op jit(solution)/shard_map/pctb,pbd->pctd/dot_general | solution.py:77
  635.9 15.2 %copy.10 = f32[4,8,128,1024]{3,1,2,0:T(8,128)S(1)} copy(f32[4,8,128,1024]{3,2,1,0:T(8,128)} %bitcast.78) | data formatting | bytes 33554432
  651.1 8.1 %fusion.16 = f32[16,131072]{1,0:T(8,128)} fusion(f32[32,131072]{1,0:T(8,128)S(1)} %bitcast.75, s32[32]{0:T(128)S(1)} %all_to_all.13), kind=kOutput, calls=%fused_computation.33 | convolution fusion | flops 805306880 | bytes 25165952 | tf_op jit(solution)/shard_map/dot_general | solution.py:86
  659.3 6.2 reshape.208
  665.5 14.5 %fusion.11 = bf16[1024,1024]{1,0:T(8,128)(2,1)} fusion(bf16[3072,1024]{1,0:T(8,128)(2,1)} %copy-done.1, f32[3072,1024]{1,0:T(8,128)} %copy-done, f32[1024]{0:T(1024)S(1)} %get-tuple-element.10, s32[1024]{0:T(1024)S(1)} %fusion.17), kind=kOutput, calls=%fused_computation.23 | convolution fusion | flops 6462373888 | bytes 20979712 | tf_op jit(solution)/shard_map/dot_general | solution.py:32
  679.9 56.3 %reduce-scatter.2.cloned.1.call-done = f32[512,1024]{1,0:T(8,128)} async-done(((f32[2048,1024]{1,0:T(8,128)}), f32[512,1024]{1,0:T(8,128)}) %reduce-scatter.2.cloned.1.call-update) | async-done | bytes 2097168 | tf_op jit(solution)/shard_map/reduce_scatter | solution.py:93
  (30 shorter events, 0.6 us)
Async XLA Ops:
  9.5 13.7 %all-to-all-start = ((s32[8,4,1]{1,2,0:T(1,128)}), s32[8,4,1]{1,2,0:T(1,128)S(1)}, u32[]{:S(2)}, u32[]{:S(2)}) async-start(s32[8,4,1]{1,2,0:T(1,128)} %bitcast.6), calls=%async_computation | async-start | bytes 8192 | tf_op jit(solution)/shard_map/all_to_all | solution.py:65
  39.3 6.4 copy-start.4
  39.3 6.6 copy-start.3
  39.3 348.4 %all-to-all-start.1 = ((bf16[32,128,1024]{2,1,0:T(8,128)(2,1)}), bf16[32,128,1024]{2,1,0:T(8,128)(2,1)}, u32[]{:S(2)}, u32[]{:S(2)}) async-start(bf16[32,128,1024]{2,1,0:T(8,128)(2,1)} %select_select_fusion.1), calls=%async_computation.1 | async-start | bytes 16777216 | tf_op jit(solution)/shard_map/all_to_all | solution.py:69
  45.0 392.1 %all-gather.2.cloned.1.call-start = ((), (), s32[]{:S(2)}) async-start(), calls=%async_computation.4 | async-start | bytes 18874368 | tf_op jit(solution)/shard_map/all_gather | solution.py:64
  395.8 4.0 copy-start.2
  399.8 6.8 copy-start.1
  406.6 9.9 %copy-start = (f32[3072,1024]{1,0:T(8,128)}, f32[3072,1024]{1,0:T(8,128)S(1)}, u32[]{:S(2)}) copy-start(f32[3072,1024]{1,0:T(8,128)S(1)} %get-tuple-element.16) | copy-start | bytes 37748740
  431.9 184.7 %all-to-all-start.2 = ((bf16[32,128,1024]{2,1,0:T(8,128)(2,1)}), bf16[32,128,1024]{2,1,0:T(8,128)(2,1)}, u32[]{:S(2)}, u32[]{:S(2)}) async-start(bf16[32,128,1024]{2,1,0:T(8,128)(2,1)} %select_select_fusion), calls=%async_computation.2 | async-start | bytes 16777216 | tf_op jit(solution)/shard_map/all_to_all | solution.py:76
  437.1 299.2 %reduce-scatter.2.cloned.1.call-start = ((), (), s32[]{:S(2)}) async-start(), calls=%async_computation.5 | async-start | bytes 10485760 | tf_op jit(solution)/shard_map/reduce_scatter | solution.py:93
Sparse Core Ops, SparseCore 0:
  47.9 388.1 all-gather.1
  665.6 70.6 reduce-scatter.1
where the time goes:
time: 744 us; the launch traced here: 743 us
  waiting for transfers between devices  579 us (78%)
  matrix products  48.7 us (7%)
  local copies, waits for them, and re-layouts  45.9 us (6%)
  other arithmetic  37.5 us (5%)
  starting transfers between devices  18.2 us (2%)
  between operations  14.2 us (2%)
    all_to_all x1, waiting for transfers between devices, body(): lax.all_to_all(outgoing, 'proto', split_axis=0, concat_axis=0, tiled=True)  342 us
    all_to_all x1, waiting for transfers between devices, body(): lax.all_to_all(outgoing_slab, 'proto', split_axis=0, concat_axis=0, tiled...  179 us
    reduce_scatter x1, waiting for transfers between devices, body(): lax.psum_scatter(summed, 'design', scatter_dimension=0, tiled=True)  56.3 us
    dot_general x1, matrix products, body(): jnp.einsum('pctb,pbd->pctd', received.reshape(proto_count, capacity, TILE...  19.3 us
    unnamed x11, local copies, waits for them, and re-layouts  15.2 us
  transfers between devices with their start and end apart: 5, of which 4 were waited for; matrix products, arithmetic and copies ran while one was open for 9% of the time, Pallas kernels for 0%

commit v1 on v0

--- a/solution.py
+++ b/solution.py
@@ -66,7 +66,22 @@
     proto_table = prototypes.astype(jnp.bfloat16).reshape(blocks_dev, TILE, feature_width)
     fetched = jnp.take(proto_table, jnp.maximum(incoming, 0), axis=0)
     outgoing = jnp.where((incoming >= 0)[:, None, None], fetched, jnp.zeros((), jnp.bfloat16))
-    arrived = lax.all_to_all(outgoing, "proto", split_axis=0, concat_axis=0, tiled=True)
+    x_now, w2 = (lax.axis_size("proto"), lax.axis_index("proto"))
+    res = list(outgoing.shape)
+    step_out = outgoing.shape[0] // x_now
+    res[0] = step_out
+    w1 = res[0]
+    res[0] = w1 * x_now
+    pp = 0
+    arrived = jnp.zeros(res, outgoing.dtype)
+    while pp < x_now:
+        top = lax.dynamic_slice_in_dim(outgoing, (w2 ^ pp) * step_out, step_out, axis=0)
+        if pp:
+            top = lax.ppermute(
+                top, axis_name="proto", perm=[(src_i, src_i ^ pp) for src_i in range(x_now)]
+            )
+        arrived = lax.dynamic_update_slice_in_dim(arrived, top, (w2 ^ pp) * w1, axis=0)
+        pp += 1
     cand_rows = jnp.take(arrived, slot_of, axis=0).reshape(cand_count * TILE, feature_width)
     losses, design_grad, logit_grad = contrast(designs, cand_rows, own_list, positives)
     slab_rows = logit_grad.T.reshape(cand_count, TILE, design_count)

time: 744 us -> 744 us (level)
  waiting for transfers between devices: 579 us -> 281 us
  blocking collectives: 0 us -> 277 us
  local copies, waits for them, and re-layouts: 45.9 us -> 62.1 us
    all_to_all x2 -> x0, waiting for transfers between devices: 521 us -> none  [the longest x1 342 us: body(): lax.all_to_all(outgoing, 'proto', split_axis=0, concat_axis=0, tiled=True)]
    all_to_all x0 -> x1, blocking collectives: none -> 277 us  [body(): lax.all_to_all(outgoing_slab, 'proto', split_axis=0, concat_axis=0, tiled...]
    ppermute x0 -> x7, waiting for transfers between devices: none -> 224 us  [body(): lax.ppermute(top, axis_name='proto', perm=[(src_i, src_i ^ pp) for src_i...]
    ppermute x0 -> x7, starting transfers between devices: none -> 14.4 us  [body(): lax.ppermute(top, axis_name='proto', perm=[(src_i, src_i ^ pp) for src_i...]
    all_to_all x2 -> x0, starting transfers between devices: 10.9 us -> none  [the longest x1 5.71 us: body(): lax.all_to_all(outgoing, 'proto', split_axis=0, concat_axis=0, tiled=True)]
    dynamic_update_slice x0 -> x7, local copies, waits for them, and re-layouts: none -> 7.45 us  [body(): lax.dynamic_update_slice_in_dim(arrived, top, (w2 ^ pp) * w1, axis=0)]
    unnamed x11 -> x13, local copies, waits for them, and re-layouts: 15.2 us -> 16.3 us
  transfers between devices with their start and end apart: 5 -> 10, of which waited for: 4 -> 6; matrix products, arithmetic and copies ran while one was open for 9% -> 13% of each run, Pallas kernels for 0% -> 0%
where the time goes in v1:
time: 744 us
  waiting for transfers between devices  281 us (38%)
  blocking collectives  277 us (37%)
  local copies, waits for them, and re-layouts  62.1 us (8%)
  matrix products  48.7 us (7%)
  other arithmetic  38.4 us (5%)
  starting transfers between devices  21.7 us (3%)
  between operations  14.2 us (2%)
    all_to_all x1, blocking collectives, body(): lax.all_to_all(outgoing_slab, 'proto', split_axis=0, concat_axis=0, tiled...  277 us
    ppermute x7, waiting for transfers between devices, body(): lax.ppermute(top, axis_name='proto', perm=[(src_i, src_i ^ pp) for src_i...  224 us
    reduce_scatter x1, waiting for transfers between devices, body(): lax.psum_scatter(summed, 'design', scatter_dimension=0, tiled=True)  56.6 us
    dot_general x1, matrix products, body(): jnp.einsum('pctb,pbd->pctd', received.reshape(proto_count, capacity, TILE...  19.3 us
    unnamed x13, local copies, waits for them, and re-layouts  16.3 us
  transfers between devices with their start and end apart: 10, of which 6 were waited for; matrix products, arithmetic and copies ran while one was open for 13% of the time, Pallas kernels for 0%

profile of v1, /device:TPU:0, one launch (start us, length us, event | category | flops | bytes accessed | tf_op | source)
XLA Modules:
  0.0 743.8 jit_solution(7865465587034532176)
XLA Ops:
  10.2 7.3 all-to-all-start
  17.6 6.7 convert_element_type.19
  25.6 7.2 gather_fusion
  32.8 7.6 %select_select_fusion.1 = bf16[32,128,1024]{2,1,0:T(8,128)(2,1)} fusion(bf16[32,128,1024]{2,1,0:T(8,128)(2,1)} %gather_fusion, pred[32]{0:T(512)(128)(4,1)S(1)} %get-tuple-element.20, pred[32]{0:T(512)(128)(4,1)S(1)} %get-tuple-element.19), kind=kLoop, calls=%fused_computation.17 | loop fusion | flops 8388608 | bytes 16777280 | tf_op jit(solution)/shard_map/jit(_where)/select_n | solution.py:68
  40.5 5.3 broadcast_in_dim.118
  45.8 1.1 copy-done.1
  46.9 2.5 constant_dynamic-slice_fusion
  49.4 2.1 collective-permute-start
  51.5 1.4 collective-permute-start.1
  53.2 2.8 collective-permute-start.3
  56.0 1.6 collective-permute-start.4
  57.6 16.3 %collective-permute-done = bf16[4,128,1024]{2,1,0:T(8,128)(2,1)S(1)} collective-permute-done((bf16[4,128,1024]{2,1,0:T(8,128)(2,1)S(1)}, bf16[4,128,1024]{2,1,0:T(8,128)(2,1)S(1)}, u32[]{:S(2)}, u32[]{:S(2)}) %collective-permute-start) | collective-permute-done | bytes 1048608 | tf_op jit(solution)/shard_map/ppermute | solution.py:80
  73.9 3.2 collective-permute-start.5
  77.2 83.3 %collective-permute-done.1 = bf16[4,128,1024]{2,1,0:T(8,128)(2,1)S(1)} collective-permute-done((bf16[4,128,1024]{2,1,0:T(8,128)(2,1)S(1)}, bf16[4,128,1024]{2,1,0:T(8,128)(2,1)S(1)}, u32[]{:S(2)}, u32[]{:S(2)}) %collective-permute-start.1) | collective-permute-done | bytes 1048608 | tf_op jit(solution)/shard_map/ppermute | solution.py:80
  160.5 3.1 collective-permute-start.6
  165.9 43.0 %collective-permute-done.2 = bf16[4,128,1024]{2,1,0:T(8,128)(2,1)S(1)} collective-permute-done((bf16[4,128,1024]{2,1,0:T(8,128)(2,1)S(1)}, bf16[4,128,1024]{2,1,0:T(8,128)(2,1)S(1)}, u32[]{:S(2)}, u32[]{:S(2)}) %collective-permute-start.2) | collective-permute-done | bytes 1048608 | tf_op jit(solution)/shard_map/ppermute | solution.py:80
  212.0 37.3 %collective-permute-done.5 = bf16[4,128,1024]{2,1,0:T(8,128)(2,1)S(1)} collective-permute-done((bf16[4,128,1024]{2,1,0:T(8,128)(2,1)S(1)}, bf16[4,128,1024]{2,1,0:T(8,128)(2,1)S(1)}, u32[]{:S(2)}, u32[]{:S(2)}) %collective-permute-start.5) | collective-permute-done | bytes 1048608 | tf_op jit(solution)/shard_map/ppermute | solution.py:80
  250.4 44.1 %collective-permute-done.6 = bf16[4,128,1024]{2,1,0:T(8,128)(2,1)S(1)} collective-permute-done((bf16[4,128,1024]{2,1,0:T(8,128)(2,1)S(1)}, bf16[4,128,1024]{2,1,0:T(8,128)(2,1)S(1)}, u32[]{:S(2)}, u32[]{:S(2)}) %collective-permute-start.6) | collective-permute-done | bytes 1048608 | tf_op jit(solution)/shard_map/ppermute | solution.py:80
  295.6 7.9 %gather_fusion.1 = bf16[24,128,1024]{2,1,0:T(8,128)(2,1)} fusion(bf16[32,128,1024]{2,1,0:T(8,128)(2,1)} %constant_dynamic-update-slice_fusion, s32[1024]{0:T(1024)S(1)} %pad_clamp_fusion.1), kind=kCustom, calls=%fused_computation.1 | custom fusion | bytes 12583008 | tf_op jit(solution)/shard_map/jit(_take)/gather | solution.py:85
  303.5 4.2 bitcast_select_fusion.1
  307.7 6.8 multiply_reduce_fusion
  314.5 3.6 fusion.2
  319.2 5.1 subtract_convert_fusion
  324.4 7.8 %gather_fusion.2 = bf16[32,128,1024]{2,1,0:T(8,128)(2,1)} fusion(bf16[24,128,1024]{2,1,0:T(8,128)(2,1)} %bitcast.77, s32[1024]{0:T(1024)S(1)} %pad_clamp_fusion), kind=kCustom, calls=%fused_computation.2 | custom fusion | bytes 16777344 | tf_op jit(solution)/shard_map/jit(_take)/gather | solution.py:89
  332.2 7.6 %select_select_fusion = bf16[32,128,1024]{2,1,0:T(8,128)(2,1)} fusion(bf16[32,128,1024]{2,1,0:T(8,128)(2,1)} %gather_fusion.2, pred[32]{0:T(512)(128)(4,1)S(1)} %get-tuple-element.25, pred[32]{0:T(512)(128)(4,1)S(1)} %fusion.14), kind=kLoop, calls=%fused_computation.16 | loop fusion | flops 8388608 | bytes 16777280 | tf_op jit(solution)/shard_map/jit(_where)/select_n | solution.py:88
  339.8 277.3 %all_to_all.14 = bf16[32,128,1024]{2,1,0:T(8,128)(2,1)} all-to-all(bf16[32,128,1024]{2,1,0:T(8,128)(2,1)} %select_select_fusion), channel_id=1, replica_groups=mesh['proto'=8,'design'=4] {'proto'}, dimensions={0} | all-to-all | bytes 16777216 | tf_op jit(solution)/shard_map/all_to_all | solution.py:91
  617.1 19.3 %fusion.29 = f32[8,4,128,1024]{3,2,1,0:T(8,128)} fusion(bf16[8,4,128,1024]{3,2,1,0:T(8,128)(2,1)} %bitcast.79, bf16[8,1024,1024,1]{2,1,3,0:T(8,128)(2,1)} %bitcast.81), kind=kOutput, calls=%fused_computation.98 | convolution fusion | flops 8589934592 | bytes 41943040 | tf_op jit(solution)/shard_map/pctb,pbd->pctd/dot_general | solution.py:92
  636.4 15.2 %copy.10 = f32[4,8,128,1024]{3,1,2,0:T(8,128)S(1)} copy(f32[4,8,128,1024]{3,2,1,0:T(8,128)} %bitcast.78) | data formatting | bytes 33554432
  651.6 8.1 %fusion.16 = f32[16,131072]{1,0:T(8,128)} fusion(f32[32,131072]{1,0:T(8,128)S(1)} %bitcast.75, s32[32]{0:T(128)S(1)} %all_to_all.10), kind=kOutput, calls=%fused_computation.34 | convolution fusion | flops 805306880 | bytes 25165952 | tf_op jit(solution)/shard_map/dot_general | solution.py:101
  659.7 6.2 reshape.208
  665.9 14.4 %fusion.11 = bf16[1024,1024]{1,0:T(8,128)(2,1)} fusion(bf16[3072,1024]{1,0:T(8,128)(2,1)} %copy-done.2, f32[3072,1024]{1,0:T(8,128)} %copy-done, f32[1024]{0:T(1024)S(1)} %get-tuple-element.10, s32[1024]{0:T(1024)S(1)} %fusion.17), kind=kOutput, calls=%fused_computation.23 | convolution fusion | flops 6462373888 | bytes 20979712 | tf_op jit(solution)/shard_map/dot_general | solution.py:32
  680.4 56.6 %reduce-scatter.2.cloned.1.call-done = f32[512,1024]{1,0:T(8,128)} async-done(((f32[2048,1024]{1,0:T(8,128)}), f32[512,1024]{1,0:T(8,128)}) %reduce-scatter.2.cloned.1.call-update) | async-done | bytes 2097168 | tf_op jit(solution)/shard_map/reduce_scatter | solution.py:108
  (51 shorter events, 13.5 us)
Async XLA Ops:
  7.2 17.1 %copy-start.4 = (s32[1024]{0:T(1024)S(1)}, s32[1024]{0:T(1024)}, u32[]{:S(2)}) copy-start(s32[1024]{0:T(1024)} %param.7) | copy-start | bytes 12292
  7.2 609.9 %all-gather.2.cloned.1.call-start = ((), (), s32[]{:S(2)}) async-start(), calls=%async_computation.3 | async-start | bytes 18874368 | tf_op jit(solution)/shard_map/all_gather | solution.py:64
  10.2 14.0 %all-to-all-start = ((s32[8,4,1]{1,2,0:T(1,128)}), s32[8,4,1]{1,2,0:T(1,128)S(1)}, u32[]{:S(2)}, u32[]{:S(2)}) async-start(s32[8,4,1]{1,2,0:T(1,128)} %bitcast.6), calls=%async_computation | async-start | bytes 8192 | tf_op jit(solution)/shard_map/all_to_all | solution.py:65
  17.5 719.5 %reduce-scatter.2.cloned.1.call-start = ((), (), s32[]{:S(2)}) async-start(), calls=%async_computation.4 | async-start | bytes 10485760 | tf_op jit(solution)/shard_map/reduce_scatter | solution.py:108
  40.5 6.4 copy-start.1
  46.9 4.6 copy-start.5
  49.4 24.5 %collective-permute-start = (bf16[4,128,1024]{2,1,0:T(8,128)(2,1)S(1)}, bf16[4,128,1024]{2,1,0:T(8,128)(2,1)S(1)}, u32[]{:S(2)}, u32[]{:S(2)}) collective-permute-start(bf16[4,128,1024]{2,1,0:T(8,128)(2,1)S(1)} %get-tuple-element.17), channel_id=1, source_target_pairs={{0,4},{4,0},{8,12},{12,8},{16,20},{20,16},{24,28},{28,24},{1,5},{5... | collective-permute-start | bytes 3145736 | tf_op jit(solution)/shard_map/ppermute | solution.py:80
  51.5 109.0 %collective-permute-start.1 = (bf16[4,128,1024]{2,1,0:T(8,128)(2,1)S(1)}, bf16[4,128,1024]{2,1,0:T(8,128)(2,1)S(1)}, u32[]{:S(2)}, u32[]{:S(2)}) collective-permute-start(bf16[4,128,1024]{2,1,0:T(8,128)(2,1)S(1)} %get-tuple-element.16), channel_id=1, source_target_pairs={{0,8},{4,12},{8,0},{12,4},{16,24},{20,28},{24,16},{28,20},{1,9},{5... | collective-permute-start | bytes 3145736 | tf_op jit(solution)/shard_map/ppermute | solution.py:80
  53.1 155.8 %collective-permute-start.2 = (bf16[4,128,1024]{2,1,0:T(8,128)(2,1)S(1)}, bf16[4,128,1024]{2,1,0:T(8,128)(2,1)S(1)}, u32[]{:S(2)}, u32[]{:S(2)}) collective-permute-start(bf16[4,128,1024]{2,1,0:T(8,128)(2,1)S(1)} %get-tuple-element.15), channel_id=1, source_target_pairs={{0,12},{4,8},{8,4},{12,0},{16,28},{20,24},{24,20},{28,16},{1,13},{... | collective-permute-start | bytes 3145736 | tf_op jit(solution)/shard_map/ppermute | solution.py:80
  53.2 156.7 %collective-permute-start.3 = (bf16[4,128,1024]{2,1,0:T(8,128)(2,1)S(1)}, bf16[4,128,1024]{2,1,0:T(8,128)(2,1)S(1)}, u32[]{:S(2)}, u32[]{:S(2)}) collective-permute-start(bf16[4,128,1024]{2,1,0:T(8,128)(2,1)S(1)} %get-tuple-element.14), channel_id=1, source_target_pairs={{0,16},{4,20},{8,24},{12,28},{16,0},{20,4},{24,8},{28,12},{1,17},{... | collective-permute-start | bytes 3145736 | tf_op jit(solution)/shard_map/ppermute | solution.py:80
  56.0 154.9 %collective-permute-start.4 = (bf16[4,128,1024]{2,1,0:T(8,128)(2,1)S(1)}, bf16[4,128,1024]{2,1,0:T(8,128)(2,1)S(1)}, u32[]{:S(2)}, u32[]{:S(2)}) collective-permute-start(bf16[4,128,1024]{2,1,0:T(8,128)(2,1)S(1)} %get-tuple-element.13), channel_id=1, source_target_pairs={{0,20},{4,16},{8,28},{12,24},{16,4},{20,0},{24,12},{28,8},{1,21},{... | collective-permute-start | bytes 3145736 | tf_op jit(solution)/shard_map/ppermute | solution.py:80
  73.9 175.5 %collective-permute-start.5 = (bf16[4,128,1024]{2,1,0:T(8,128)(2,1)S(1)}, bf16[4,128,1024]{2,1,0:T(8,128)(2,1)S(1)}, u32[]{:S(2)}, u32[]{:S(2)}) collective-permute-start(bf16[4,128,1024]{2,1,0:T(8,128)(2,1)S(1)} %get-tuple-element.12), channel_id=1, source_target_pairs={{0,24},{4,28},{8,16},{12,20},{16,8},{20,12},{24,0},{28,4},{1,25},{... | collective-permute-start | bytes 3145736 | tf_op jit(solution)/shard_map/ppermute | solution.py:80
  160.5 134.1 %collective-permute-start.6 = (bf16[4,128,1024]{2,1,0:T(8,128)(2,1)S(1)}, bf16[4,128,1024]{2,1,0:T(8,128)(2,1)S(1)}, u32[]{:S(2)}, u32[]{:S(2)}) collective-permute-start(bf16[4,128,1024]{2,1,0:T(8,128)(2,1)S(1)} %get-tuple-element.11), channel_id=1, source_target_pairs={{0,28},{4,24},{8,20},{12,16},{16,12},{20,8},{24,4},{28,0},{1,29},{... | collective-permute-start | bytes 3145736 | tf_op jit(solution)/shard_map/ppermute | solution.py:80
  303.5 4.2 copy-start.3
  307.7 6.8 copy-start.2
  314.5 9.9 %copy-start = (f32[3072,1024]{1,0:T(8,128)}, f32[3072,1024]{1,0:T(8,128)S(1)}, u32[]{:S(2)}) copy-start(f32[3072,1024]{1,0:T(8,128)S(1)} %get-tuple-element.24) | copy-start | bytes 37748740
Sparse Core Ops, SparseCore 0:
  10.1 399.7 all-gather.1
  666.0 70.9 reduce-scatter.1
